TPU v7x, 32 devices: a whole 2x2x4 slice. The times are simulated.
32 devices in a mesh: rows: 16 (over z, y, x), cols: 2 (over core).
Axes of the slice: x: 2, y: 2, z: 4, core: 2. Of those that a mesh axis runs over, the one named last changes fastest.
Arguments:
- tokens_in: bfloat16 [6304, 768], P(('rows', 'cols')), may hold values from -6 to 6
- ln1_gain: float32 [768], replicated, may hold values from 0.5 to 1.5
- ln1_shift: float32 [768], replicated, may hold values from -4 to 4
- qkv_weight: bfloat16 [768, 2304], P(None, 'cols'), may hold values from -0.21875 to 0.21875
- out_weight: bfloat16 [768, 768], P('cols'), may hold values from -1.75 to 1.75
- ln2_gain: float32 [768], replicated, may hold values from 0.5 to 1.5
- ln2_shift: float32 [768], replicated, may hold values from -4 to 4
- router_weight: bfloat16 [768, 32], replicated, may hold values from -0.4375 to 0.4375
- expert_in: bfloat16 [768, 98304], P(None, ('rows', 'cols')), may hold values from -0.21875 to 0.21875
- expert_out: bfloat16 [98304, 768], P(('rows', 'cols')), may hold values from -0.4375 to 0.4375
- routes: int32 [6304, 2], P(('rows', 'cols')), may hold values from 0 to 31, all different within a row; in each aligned block of 197 rows (0 to 196, 197 to 393, ...) at most 16 rows name the same one
- cotangent: bfloat16 [6304, 768], P(('rows', 'cols')), may hold values from -6 to 6
Outputs:
- output: bfloat16 [6304, 768], P(('rows', 'cols'))
- tokens_grad: bfloat16 [6304, 768], P(('rows', 'cols'))
- ln1_gain_grad: float32 [768], replicated
- ln1_shift_grad: float32 [768], replicated
- qkv_grad: float32 [768, 2304], P(None, 'cols')
- out_grad: float32 [768, 768], P('cols')
- ln2_gain_grad: float32 [768], replicated
- ln2_shift_grad: float32 [768], replicated
- router_grad: float32 [768, 32], replicated
- expert_in_grad: float32 [768, 98304], P(None, ('rows', 'cols'))
- expert_out_grad: float32 [98304, 768], P(('rows', 'cols'))
Inputs may be any that keep to these rules, and one draw needn't show every extreme that they name: `routes`: the two experts of a token differ. Among the tokens of one device (aligned blocks of 197 rows) each expert is named by at most 16 assignments, a bound that some block reaches.
All inputs are finite; a program needn't handle non-finite values.
Results may differ from a plain program's by a relative error of at most 0.022.
Values may be sent and summed in bfloat16 or wider, within the bound.
A program may use at most 192 MiB of HBM per device.

v0:
```python
import jax
import jax.numpy as jnp
from jax import lax
from jax.sharding import PartitionSpec as P

DH = 64
FF = 3072
SEQ = 197
EPSILON = 1e-06


def layer_norm(values, norm_gain, norm_shift):
    average = jnp.mean(values, axis=-1, keepdims=True)
    centred = values - average
    variance = jnp.mean(centred * centred, axis=-1, keepdims=True)
    return centred * lax.rsqrt(variance + EPSILON) * norm_gain + norm_shift


def gelu_slope(pre_act):
    normal_cdf = 0.5 * (1.0 + jax.scipy.special.erf(pre_act * 0.7071067811865476))
    density = jnp.exp(-0.5 * pre_act * pre_act) * 0.3989422804014327
    return normal_cdf + pre_act * density


def dot_rows(first_side, second_side):
    return lax.dot_general(
        first_side, second_side, (((0,), (0,)), ((), ())), preferred_element_type=jnp.float32
    )


def dot_last(first_side, second_side):
    return lax.dot_general(
        first_side, second_side, (((1,), (1,)), ((), ())), preferred_element_type=jnp.float32
    )


def attention_scores(queries, keys_all, score_scale):
    scores = jnp.einsum("nqhd,nkhd->nhqk", queries, keys_all, preferred_element_type=jnp.float32)
    return scores * score_scale


def body(
    tokens_in,
    ln1_gain,
    ln1_shift,
    qkv_weight,
    out_weight,
    ln2_gain,
    ln2_shift,
    router_weight,
    expert_in,
    expert_out,
    routes,
    cotangent,
):
    local_rows = tokens_in.shape[0]
    model_width = tokens_in.shape[1]
    experts = router_weight.shape[1]
    capacity = max(2, 8 * local_rows // (3 * experts))
    heads_local = qkv_weight.shape[1] // (3 * DH)
    score_scale = DH ** (-0.5)
    row_count = lax.axis_size("rows")
    row_place = lax.axis_index("rows")
    col_place = lax.axis_index("cols")
    per_device = max(1, experts // row_count)
    copies = max(1, row_count // experts)
    slots = per_device * capacity
    piece_half = expert_in.shape[1]
    piece_whole = piece_half * lax.axis_size("cols")
    arrived_rows = row_count * slots
    tokens_f = tokens_in.astype(jnp.float32)
    normed_low = layer_norm(tokens_f, ln1_gain, ln1_shift).astype(jnp.bfloat16)
    gathered = lax.all_gather(normed_low, "cols", axis=0, tiled=True)
    pair_rows = gathered.shape[0]
    images = pair_rows // SEQ
    qkv_low = jnp.dot(gathered, qkv_weight, preferred_element_type=jnp.float32).astype(jnp.bfloat16)
    head_split = qkv_low.reshape(images, SEQ, heads_local, 3, DH)
    queries = head_split[:, :, :, 0]
    keys_all = head_split[:, :, :, 1]
    values_all = head_split[:, :, :, 2]
    scores = attention_scores(queries, keys_all, score_scale)
    score_peak = jnp.max(scores, axis=-1, keepdims=True)
    log_total = score_peak + jnp.log(jnp.sum(jnp.exp(scores - score_peak), axis=-1, keepdims=True))
    weights_low = jnp.exp(scores - log_total).astype(jnp.bfloat16)
    context = jnp.einsum(
        "nhqk,nkhd->nqhd", weights_low, values_all, preferred_element_type=jnp.float32
    )
    context_low = context.astype(jnp.bfloat16).reshape(pair_rows, heads_local * DH)
    row_block = context_low
    attn_out = lax.psum_scatter(
        jnp.dot(row_block, out_weight, preferred_element_type=jnp.float32),
        "cols",
        scatter_dimension=0,
        tiled=True,
    )
    hidden_one = tokens_f + attn_out
    mixed_low = layer_norm(hidden_one, ln2_gain, ln2_shift).astype(jnp.bfloat16)
    logits = jnp.dot(mixed_low, router_weight, preferred_element_type=jnp.float32)
    router_probs = jax.nn.softmax(logits, axis=-1)
    expert_ids = jnp.arange(experts, dtype=jnp.int32)
    chosen = (routes[:, :, None] == expert_ids[None, None, :]).astype(jnp.float32)
    gate_values = jnp.sum(router_probs[:, None, :] * chosen, axis=-1)
    flat_ids = routes.reshape(-1)
    flat_hot = (flat_ids[:, None] == expert_ids[None, :]).astype(jnp.int32)
    slot_ranks = jnp.sum(jnp.cumsum(flat_hot, axis=0) * flat_hot, axis=1) - 1
    first_device = flat_ids // per_device * copies
    slot_index = flat_ids % per_device * capacity + slot_ranks
    copy_ids = jnp.arange(copies, dtype=jnp.int32)
    targets = ((first_device[:, None] + copy_ids[None, :]) * slots + slot_index[:, None]).reshape(
        -1
    )
    grad_out = cotangent.astype(jnp.float32)
    grad_slots = (
        (gate_values[:, :, None] * grad_out[:, None, :])
        .astype(jnp.bfloat16)
        .reshape(2 * local_rows, model_width)
    )
    rows_send = (
        jnp.zeros((arrived_rows, model_width), jnp.bfloat16)
        .at[targets]
        .set(jnp.repeat(mixed_low, 2 * copies, axis=0))
    )
    grads_send = (
        jnp.zeros((arrived_rows, model_width), jnp.bfloat16)
        .at[targets]
        .set(jnp.repeat(grad_slots, copies, axis=0))
    )
    arrived, grad_result = (
        lax.all_to_all(
            rows_send.reshape(row_count, slots, model_width),
            "rows",
            split_axis=0,
            concat_axis=0,
            tiled=True,
        ),
        lax.all_to_all(
            grads_send.reshape(row_count, slots, model_width),
            "rows",
            split_axis=0,
            concat_axis=0,
            tiled=True,
        ),
    )
    arrived = arrived.reshape(arrived_rows, model_width)
    grad_result = grad_result.reshape(arrived_rows, model_width)
    unit_base = row_place % copies * piece_whole
    both_rows, both_grads = (
        lax.all_gather(arrived, "cols", axis=0, tiled=True),
        lax.all_gather(grad_result, "cols", axis=0, tiled=True),
    )
    slot_local = jnp.arange(both_rows.shape[0], dtype=jnp.int32) % slots // capacity
    unit_local = (
        unit_base + col_place * piece_half + jnp.arange(piece_half, dtype=jnp.int32)
    ) // FF
    mask = (slot_local[:, None] == unit_local[None, :]).astype(jnp.float32)
    pre_act = jnp.dot(both_rows, expert_in, preferred_element_type=jnp.float32) * mask
    act_low = jax.nn.gelu(pre_act, approximate=False).astype(jnp.bfloat16)
    result_low = lax.psum_scatter(
        jnp.dot(act_low, expert_out, preferred_element_type=jnp.float32).astype(jnp.bfloat16),
        "cols",
        scatter_dimension=0,
        tiled=True,
    )
    grad_act = dot_last(both_grads, expert_out)
    grad_pre_low = (grad_act * gelu_slope(pre_act) * mask).astype(jnp.bfloat16)
    first_grad = dot_rows(both_rows, grad_pre_low)
    second_grad = dot_rows(act_low, both_grads)
    grad_arrived = lax.psum_scatter(
        dot_last(grad_pre_low, expert_in).astype(jnp.bfloat16),
        "cols",
        scatter_dimension=0,
        tiled=True,
    )
    returned = lax.all_to_all(
        result_low.reshape(row_count, slots, model_width),
        "rows",
        split_axis=0,
        concat_axis=0,
        tiled=True,
    )
    returned = returned.reshape(arrived_rows, model_width)
    picked = jnp.sum(
        returned[targets].reshape(local_rows, 2, copies, model_width).astype(jnp.float32), axis=2
    )
    output = (hidden_one + jnp.sum(gate_values[:, :, None] * picked, axis=1)).astype(jnp.bfloat16)
    grad_gates = jnp.sum(grad_out[:, None, :] * picked, axis=-1)
    grad_sent = lax.all_to_all(
        grad_arrived.reshape(row_count, slots, model_width),
        "rows",
        split_axis=0,
        concat_axis=0,
        tiled=True,
    )
    grad_sent = grad_sent.reshape(arrived_rows, model_width)
    grad_mixed_experts = jnp.sum(
        grad_sent[targets].reshape(local_rows, 2 * copies, model_width).astype(jnp.float32), axis=1
    )
    gate_term = jnp.sum(grad_gates * gate_values, axis=-1, keepdims=True)
    grad_probs = jnp.sum(chosen * grad_gates[:, :, None], axis=1)
    grad_logits_low = (router_probs * (grad_probs - gate_term)).astype(jnp.bfloat16)
    router_grad = dot_rows(mixed_low, grad_logits_low)
    grad_mixed = dot_last(grad_logits_low, router_weight) + grad_mixed_experts
    unused_two, norm_two_back = jax.vjp(layer_norm, hidden_one, ln2_gain, ln2_shift)
    grad_hidden_part, ln2_gain_grad, ln2_shift_grad = norm_two_back(grad_mixed)
    grad_hidden = grad_out + grad_hidden_part
    grad_attn_low = grad_hidden.astype(jnp.bfloat16)
    grad_attn_all = lax.all_gather(grad_attn_low, "cols", axis=0, tiled=True)
    out_grad = dot_rows(context_low, grad_attn_all)
    grad_context = (
        dot_last(grad_attn_all, out_weight)
        .astype(jnp.bfloat16)
        .reshape(images, SEQ, heads_local, DH)
    )
    scores_again = attention_scores(queries, keys_all, score_scale)
    attn_probs = jnp.exp(scores_again - log_total)
    probs_low = attn_probs.astype(jnp.bfloat16)
    grad_values = jnp.einsum(
        "nhqk,nqhd->nkhd", probs_low, grad_context, preferred_element_type=jnp.float32
    )
    grad_weights = jnp.einsum(
        "nqhd,nkhd->nhqk", grad_context, values_all, preferred_element_type=jnp.float32
    )
    row_term = jnp.sum(grad_weights * attn_probs, axis=-1, keepdims=True)
    grad_scores = (attn_probs * (grad_weights - row_term)).astype(jnp.bfloat16)
    grad_queries = (
        jnp.einsum("nhqk,nkhd->nqhd", grad_scores, keys_all, preferred_element_type=jnp.float32)
        * score_scale
    )
    grad_keys = (
        jnp.einsum("nhqk,nqhd->nkhd", grad_scores, queries, preferred_element_type=jnp.float32)
        * score_scale
    )
    grad_qkv = (
        jnp.stack([grad_queries, grad_keys, grad_values], axis=3)
        .astype(jnp.bfloat16)
        .reshape(pair_rows, 3 * heads_local * DH)
    )
    qkv_grad = dot_rows(gathered, grad_qkv)
    row_block = grad_qkv
    grad_normed = lax.psum_scatter(
        dot_last(row_block, qkv_weight).astype(jnp.bfloat16),
        "cols",
        scatter_dimension=0,
        tiled=True,
    ).astype(jnp.float32)
    unused_one, norm_one_back = jax.vjp(layer_norm, tokens_f, ln1_gain, ln1_shift)
    grad_tokens_part, ln1_gain_grad, ln1_shift_grad = norm_one_back(grad_normed)
    tokens_grad = (grad_hidden + grad_tokens_part).astype(jnp.bfloat16)
    qkv_grad, out_grad = lax.psum((qkv_grad, out_grad), "rows")
    router_grad, ln1_gain_grad, ln1_shift_grad, ln2_gain_grad, ln2_shift_grad = lax.psum(
        (router_grad, ln1_gain_grad, ln1_shift_grad, ln2_gain_grad, ln2_shift_grad),
        ("rows", "cols"),
    )
    return (
        output,
        tokens_grad,
        ln1_gain_grad,
        ln1_shift_grad,
        qkv_grad,
        out_grad,
        ln2_gain_grad,
        ln2_shift_grad,
        router_grad,
        first_grad,
        second_grad,
    )


def solution(mesh):
    in_specs = (
        P(("rows", "cols"), None),
        P(),
        P(),
        P(None, "cols"),
        P("cols", None),
        P(),
        P(),
        P(),
        P(None, ("rows", "cols")),
        P(("rows", "cols"), None),
        P(("rows", "cols"), None),
        P(("rows", "cols"), None),
    )
    out_specs = (
        P(("rows", "cols"), None),
        P(("rows", "cols"), None),
        P(),
        P(),
        P(None, "cols"),
        P("cols", None),
        P(),
        P(),
        P(),
        P(None, ("rows", "cols")),
        P(("rows", "cols"), None),
    )
    return jax.shard_map(body, mesh=mesh, in_specs=in_specs, out_specs=out_specs, check_vma=False)
```

profile of v0, /device:TPU:0, one launch (start us, length us, event | category | flops | bytes accessed | tf_op | source)
XLA Modules:
  0.0 595.0 jit_solution(453533763309978735)
XLA Ops:
  11.4 2.3 all-gather
  14.9 2.8 reshape.405
  17.7 7.0 %fusion.72 = (bf16[2,197,6,1,64]{4,3,2,1,0:T(2,128)(2,1)S(1)}, bf16[2,197,6,1,64]{4,3,2,1,0:T(2,128)(2,1)}, bf16[2,197,6,1,64]{4,3,2,1,0:T(2,128)(2,1)}) fusion(bf16[2,197,6,3,64]{4,3,2,1,0:T(4,128)(2,1)} %reshape.405), kind=kLoop, calls=%fused_computation.161 | loop fusion | bytes 1815552 | tf_op jit(solution)/shard_map/slice | solution.py:78
  24.7 2.5 copy.120
  27.2 3.7 copy.122
  30.9 2.0 copy.121
  39.8 4.9 fusion
  45.4 2.0 collective-permute-start
  50.8 2.1 concatenate
  56.2 3.9 scatter_custom_fusion
  60.0 8.3 %all-to-all-start = ((bf16[16,32,768]{2,1,0:T(8,128)(2,1)}), bf16[16,32,768]{2,1,0:T(8,128)(2,1)}, u32[]{:S(2)}, u32[]{:S(2)}) async-start(bf16[16,32,768]{2,1,0:T(8,128)(2,1)} %bitcast.8), calls=%async_computation | async-start | bytes 1572864 | tf_op jit(solution)/shard_map/all_to_all | solution.py:129
  69.7 2.1 mul.309
  72.2 15.5 %all-to-all-done = bf16[16,32,768]{2,1,0:T(8,128)(2,1)} async-done(((bf16[16,32,768]{2,1,0:T(8,128)(2,1)}), bf16[16,32,768]{2,1,0:T(8,128)(2,1)}, u32[]{:S(2)}, u32[]{:S(2)}) %all-to-all-start) | async-done | bytes 786464 | tf_op jit(solution)/shard_map/all_to_all | solution.py:129
  88.0 3.2 scatter_custom_fusion.1
  91.2 4.9 all-to-all-start.2
  96.2 18.6 %all-to-all-done.2 = bf16[16,32,768]{2,1,0:T(8,128)(2,1)S(1)} async-done(((bf16[16,32,768]{2,1,0:T(8,128)(2,1)}), bf16[16,32,768]{2,1,0:T(8,128)(2,1)S(1)}, u32[]{:S(2)}, u32[]{:S(2)}) %all-to-all-start.2) | async-done | bytes 786464 | tf_op jit(solution)/shard_map/all_to_all | solution.py:136
  115.8 35.3 %fusion.5 = (bf16[1024,3072]{1,0:T(8,128)(2,1)S(1)}, f32[1024,3072]{1,0:T(8,128)}) fusion(s32[3072]{0:T(1024)S(1)} %add_select_fusion, s32[1024]{0:T(1024)S(1)} %add_select_fusion.1, bf16[1024,768]{1,0:T(8,128)(2,1)} %all-gather.5.cloned.1.call-done, bf16[768,3072]{1,0:T(8,128)(2,1)} %param.20), kind=kOutput, calls=%fused_computation.11 | convolution fusion | flops 5042601984 | bytes 25182208 | tf_op jit(solution)/shard_map/dot_general | solution.py:156
  151.1 2.7 copy-done.44
  153.8 8.5 %convolution_convert_fusion.2 = bf16[1024,768]{1,0:T(8,128)(2,1)} fusion(bf16[1024,3072]{1,0:T(8,128)(2,1)S(1)} %get-tuple-element.37, bf16[3072,768]{1,0:T(8,128)(2,1)} %param.21), kind=kOutput, calls=%fused_computation.39 | convolution fusion | flops 4832624640 | bytes 12582912 | tf_op jit(solution)/shard_map/dot_general | solution.py:159
  162.3 8.7 %reduce-scatter.9.cloned.1.call-start = ((), (), s32[]{:S(2)}) async-start(), calls=%async_computation.9 | async-start | bytes 2359296 | tf_op jit(solution)/shard_map/reduce_scatter | solution.py:168
  171.1 12.0 %fusion.2 = bf16[1024,3072]{1,0:T(8,128)(2,1)S(1)} fusion(f32[1024,3072]{1,0:T(8,128)} %get-tuple-element.38, bf16[1024,768]{1,0:T(8,128)(2,1)} %all-gather.7.cloned.1.call-done, bf16[3072,768]{1,0:T(8,128)(2,1)} %param.21, s32[3072]{0:T(1024)S(1)} %add_select_fusion, s32[1024]{0:T(1024)S(1)} %add_select_fusion.1), kind=kOutput, calls=%fused_computation.8 | convolution fusion | flops 4872732672 | bytes 25182208 | tf_op jit(solution)/shard_map/dot_general | solution.py:32
  183.1 2.7 copy-done.43
  185.8 6.3 %convolution_convert_fusion.1 = bf16[1024,768]{1,0:T(8,128)(2,1)} fusion(bf16[1024,3072]{1,0:T(8,128)(2,1)S(1)} %fusion.2, bf16[768,3072]{1,0:T(8,128)(2,1)S(1)} %bitcast.115), kind=kOutput, calls=%fused_computation.38 | convolution fusion | flops 4832624640 | bytes 12582912 | tf_op jit(solution)/shard_map/dot_general | solution.py:32
  192.1 5.2 all-to-all-start.1
  197.2 3.5 reduce-scatter.9.cloned.1.call-done
  200.8 15.2 %all-to-all-done.1 = bf16[16,32,768]{2,1,0:T(8,128)(2,1)S(1)} async-done(((bf16[16,32,768]{2,1,0:T(8,128)(2,1)}), bf16[16,32,768]{2,1,0:T(8,128)(2,1)S(1)}, u32[]{:S(2)}, u32[]{:S(2)}) %all-to-all-start.1) | async-done | bytes 786464 | tf_op jit(solution)/shard_map/all_to_all | solution.py:174
  216.0 4.9 all-to-all-start.3
  220.9 1.8 convert_element_type.105
  222.8 2.6 gather_fusion
  225.4 2.8 reshape.365
  228.2 4.7 multiply_reduce_fusion.2
  234.1 5.3 all-to-all-done.3
  239.5 2.6 gather_fusion.1
  242.1 2.8 reshape.366
  245.0 2.7 reduce_sum.212
  249.8 2.0 fusion.70
  252.8 2.6 all-gather.1
  260.9 3.2 fusion.22
  270.2 4.6 fusion.75
  276.4 10.0 %fusion.79 = f32[3072,768]{1,0:T(8,128)} fusion(bf16[1024,3072]{1,0:T(8,128)(2,1)} %copy-done.44, bf16[1024,768]{1,0:T(8,128)(2,1)} %all-gather.7.cloned.1.call-done), kind=kOutput, calls=%fused_computation.168 | convolution fusion | flops 4831838208 | bytes 17301504 | tf_op jit(solution)/shard_map/dot_general | solution.py:26
  287.7 3.4 fusion.1
  291.8 2.7 collective-permute-start.1
  294.5 9.9 %fusion.78 = f32[768,3072]{1,0:T(8,128)} fusion(bf16[1024,768]{1,0:T(8,128)(2,1)} %all-gather.5.cloned.1.call-done, bf16[1024,3072]{1,0:T(8,128)(2,1)} %copy-done.43), kind=kOutput, calls=%fused_computation.167 | convolution fusion | flops 4831838208 | bytes 17301504 | tf_op jit(solution)/shard_map/dot_general | solution.py:26
  304.4 2.0 concatenate.1
  307.3 40.2 %all-reduce.5 = (f32[768]{0:T(1024)}, f32[768]{0:T(1024)}, f32[768]{0:T(1024)}, f32[768]{0:T(1024)}) all-reduce(f32[768]{0:T(1024)S(1)} %get-tuple-element.15, f32[768]{0:T(1024)S(1)} %get-tuple-element.18, f32[768]{0:T(1024)S(1)} %get-tuple-element.11, ...), channel_id=1, replica_groups=mesh['rows'=16,'cols'=2] {'rows','cols'}, use_global_device_ids=true, to_apply=%region_29.30 | all-reduce | flops 3072 | bytes 24576 | tf_op jit(solution)/shard_map/psum | solution.py:250
  348.6 46.3 %all-reduce.10.cloned.1.call-done = f32[768,32]{0,1:T(8,128)} async-done(((f32[768,32]{0,1:T(8,128)}), f32[768,32]{0,1:T(8,128)}) %all-reduce.10.cloned.1.call-update) | async-done | bytes 98320 | tf_op jit(solution)/shard_map/psum | solution.py:250
  394.8 187.2 %all-reduce.12.cloned.1.call-done = (f32[768,1152]{1,0:T(8,128)}, f32[384,768]{1,0:T(8,128)}) async-done(((f32[768,1152]{1,0:T(8,128)}, f32[384,768]{1,0:T(8,128)}), (f32[768,1152]{1,0:T(8,128)}, f32[384,768]{1,0:T(8,128)})) %all-reduce.12.cloned.1.call-update) | async-done | bytes 4718608 | tf_op jit(solution)/shard_map/psum | solution.py:249
  582.0 4.1 copy.130
  (185 shorter events, 44.7 us)
Async XLA Ops:
  7.2 6.7 %copy-start = (bf16[768,1152]{1,0:T(8,128)(2,1)S(1)}, bf16[768,1152]{1,0:T(8,128)(2,1)}, u32[]{:S(2)}) copy-start(bf16[768,1152]{1,0:T(8,128)(2,1)} %param.15) | copy-start | bytes 5308420
  8.4 3.0 copy-start.29
  27.2 9.4 %copy-start.13 = (bf16[2,197,6,1,64]{1,4,2,0,3:T(8,128)(2,1)}, bf16[2,197,6,1,64]{1,4,2,0,3:T(8,128)(2,1)S(1)}, u32[]{:S(2)}) copy-start(bf16[2,197,6,1,64]{1,4,2,0,3:T(8,128)(2,1)S(1)} %copy.120) | copy-start | bytes 907780
  35.1 12.4 %copy-start.31 = (s32[197,2]{0,1:T(2,128)S(1)}, s32[197,2]{0,1:T(2,128)}, u32[]{:S(2)}) copy-start(s32[197,2]{0,1:T(2,128)} %param.22) | copy-start | bytes 4732
  36.0 13.5 %copy-start.42 = (u32[32]{0:T(128)S(1)}, u32[32]{0:T(128)}, u32[]{:S(2)}) copy-start(u32[32]{0:T(128)} %constant.193) | copy-start | bytes 388
  36.0 16.9 %copy-start.5 = (bf16[197,768]{1,0:T(8,128)(2,1)S(1)}, bf16[197,768]{1,0:T(8,128)(2,1)}, u32[]{:S(2)}) copy-start(bf16[197,768]{1,0:T(8,128)(2,1)} %param.12) | copy-start | bytes 907780
  37.1 16.9 %copy-start.28 = (f32[768]{0:T(1024)S(1)}, f32[768]{0:T(1024)}, u32[]{:S(2)}) copy-start(f32[768]{0:T(1024)} %param.17) | copy-start | bytes 9220
  37.1 16.9 %copy-start.41 = (f32[768]{0:T(1024)S(1)}, f32[768]{0:T(1024)}, u32[]{:S(2)}) copy-start(f32[768]{0:T(1024)} %param.18) | copy-start | bytes 9220
  45.4 5.4 collective-permute-start
  47.9 20.5 %copy-start.9 = (bf16[197,768]{1,0:T(8,128)(2,1)S(1)}, bf16[197,768]{1,0:T(8,128)(2,1)}, u32[]{:S(2)}) copy-start(bf16[197,768]{1,0:T(8,128)(2,1)} %param.23) | copy-start | bytes 907780
  53.4 18.8 %copy-start.39 = (f32[197]{0:T(256)}, f32[197]{0:T(256)S(1)}, u32[]{:S(2)}) copy-start(f32[197]{0:T(256)S(1)} %multiply_reduce_fusion.6) | copy-start | bytes 2368
  53.4 18.5 %copy-start.25 = (bf16[768,32]{0,1:T(8,128)(2,1)S(1)}, bf16[768,32]{0,1:T(8,128)(2,1)}, u32[]{:S(2)}) copy-start(bf16[768,32]{0,1:T(8,128)(2,1)} %param.19) | copy-start | bytes 147460
  53.9 18.2 %copy-start.34 = (f32[197]{0:T(256)}, f32[197]{0:T(256)S(1)}, u32[]{:S(2)}) copy-start(f32[197]{0:T(256)S(1)} %fusion.67) | copy-start | bytes 2368
  54.1 33.6 %copy-start.11 = (bf16[197,768]{1,0:T(8,128)(2,1)}, bf16[197,768]{1,0:T(8,128)(2,1)S(1)}, u32[]{:S(2)}) copy-start(bf16[197,768]{1,0:T(8,128)(2,1)S(1)} %add_convert_fusion.2) | copy-start | bytes 907780
  60.0 27.7 %all-to-all-start = ((bf16[16,32,768]{2,1,0:T(8,128)(2,1)}), bf16[16,32,768]{2,1,0:T(8,128)(2,1)}, u32[]{:S(2)}, u32[]{:S(2)}) async-start(bf16[16,32,768]{2,1,0:T(8,128)(2,1)} %bitcast.8), calls=%async_computation | async-start | bytes 1572864 | tf_op jit(solution)/shard_map/all_to_all | solution.py:129
  68.3 47.4 %all-gather.5.cloned.1.call-start = ((), (), s32[]{:S(2)}) async-start(), calls=%async_computation.6 | async-start | bytes 2359296 | tf_op jit(solution)/shard_map/all_gather | solution.py:148
  72.2 15.5 %copy-start.36 = (f32[197]{0:T(256)}, f32[197]{0:T(256)S(1)}, u32[]{:S(2)}) copy-start(f32[197]{0:T(256)S(1)} %fusion.55) | copy-start | bytes 2368
  91.2 23.5 %all-to-all-start.2 = ((bf16[16,32,768]{2,1,0:T(8,128)(2,1)}), bf16[16,32,768]{2,1,0:T(8,128)(2,1)S(1)}, u32[]{:S(2)}, u32[]{:S(2)}) async-start(bf16[16,32,768]{2,1,0:T(8,128)(2,1)} %bitcast.107), calls=%async_computation.3 | async-start | bytes 1572864 | tf_op jit(solution)/shard_map/all_to_all | solution.py:136
  96.1 74.9 %all-gather.7.cloned.1.call-start = ((), (), s32[]{:S(2)}) async-start(), calls=%async_computation.8 | async-start | bytes 2359296 | tf_op jit(solution)/shard_map/all_gather | solution.py:149
  115.7 76.4 %reduce-scatter.7.cloned.1.call-start = ((), (), s32[]{:S(2)}) async-start(), calls=%async_computation.7 | async-start | bytes 2359296 | tf_op jit(solution)/shard_map/reduce_scatter | solution.py:158
  151.0 2.7 copy-start.44
  153.8 32.0 %slice-start = ((s8[4718592]{0:T(1024)(128)(4,1)}), s8[524288]{0:T(1024)(128)(4,1)S(1)}, s32[]{:S(2)}) async-start(s8[4718592]{0:T(1024)(128)(4,1)} %bitcast.114), calls=%async_computation.12 | async-start | bytes 1048576
  162.3 38.5 %reduce-scatter.9.cloned.1.call-start = ((), (), s32[]{:S(2)}) async-start(), calls=%async_computation.9 | async-start | bytes 2359296 | tf_op jit(solution)/shard_map/reduce_scatter | solution.py:168
  171.1 14.7 %slice-start.1 = ((s8[4718592]{0:T(1024)(128)(4,1)}), s8[4194304]{0:T(1024)(128)(4,1)S(1)}, s32[]{:S(2)}) async-start(s8[4718592]{0:T(1024)(128)(4,1)} %bitcast.114), calls=%async_computation.13 | async-start | bytes 8388608
  183.1 2.7 copy-start.43
  192.1 23.9 %all-to-all-start.1 = ((bf16[16,32,768]{2,1,0:T(8,128)(2,1)}), bf16[16,32,768]{2,1,0:T(8,128)(2,1)S(1)}, u32[]{:S(2)}, u32[]{:S(2)}) async-start(bf16[16,32,768]{2,1,0:T(8,128)(2,1)} %bitcast.109), calls=%async_computation.2 | async-start | bytes 1572864 | tf_op jit(solution)/shard_map/all_to_all | solution.py:174
  216.0 23.5 %all-to-all-start.3 = ((bf16[16,32,768]{2,1,0:T(8,128)(2,1)}), bf16[16,32,768]{2,1,0:T(8,128)(2,1)S(1)}, u32[]{:S(2)}, u32[]{:S(2)}) async-start(bf16[16,32,768]{2,1,0:T(8,128)(2,1)} %bitcast.108), calls=%async_computation.5 | async-start | bytes 1572864 | tf_op jit(solution)/shard_map/all_to_all | solution.py:187
  220.9 174.0 %all-reduce.10.cloned.1.call-start = ((), (), s32[]{:S(2)}) async-start(), calls=%async_computation.10 | async-start | bytes 196608 | tf_op jit(solution)/shard_map/psum | solution.py:250
  232.8 15.6 %copy-start.4 = (f32[197,768]{1,0:T(8,128)S(1)}, f32[197,768]{1,0:T(8,128)}, u32[]{:S(2)}) copy-start(f32[197,768]{1,0:T(8,128)} %copy-done.3) | copy-start | bytes 1815556
  242.1 7.6 %copy-start.40 = (f32[197]{0:T(256)S(1)}, f32[197]{0:T(256)}, u32[]{:S(2)}) copy-start(f32[197]{0:T(256)} %copy-done.39) | copy-start | bytes 2368
  242.1 7.7 %copy-start.35 = (f32[197]{0:T(256)S(1)}, f32[197]{0:T(256)}, u32[]{:S(2)}) copy-start(f32[197]{0:T(256)} %copy-done.34) | copy-start | bytes 2368
  242.1 10.5 %copy-start.10 = (bf16[197,768]{1,0:T(8,128)(2,1)S(1)}, bf16[197,768]{1,0:T(8,128)(2,1)}, u32[]{:S(2)}) copy-start(bf16[197,768]{1,0:T(8,128)(2,1)} %param.23) | copy-start | bytes 907780
  252.8 11.3 %copy-start.14 = (bf16[2,197,6,1,64]{1,4,2,0,3:T(8,128)(2,1)S(1)}, bf16[2,197,6,1,64]{1,4,2,0,3:T(8,128)(2,1)}, u32[]{:S(2)}) copy-start(bf16[2,197,6,1,64]{1,4,2,0,3:T(8,128)(2,1)} %copy-done.13) | copy-start | bytes 907780
  260.9 3.2 copy-start.2
  264.9 2.3 copy-start.20
  270.2 4.7 copy-start.17
  270.2 4.7 copy-start.19
  274.9 307.1 %all-reduce.12.cloned.1.call-start = ((), (), s32[]{:S(2)}) async-start(), calls=%async_computation.11 | async-start | bytes 9437184 | tf_op jit(solution)/shard_map/psum | solution.py:249
  276.4 10.0 %copy-start.23 = (bf16[394,1152]{0,1:T(8,128)(2,1)S(1)}, bf16[394,1152]{0,1:T(8,128)(2,1)}, u32[]{:S(2)}) copy-start(bf16[394,1152]{0,1:T(8,128)(2,1)} %convert_element_type.115) | copy-start | bytes 2723332
  291.8 14.7 %copy-start.6 = (bf16[197,768]{1,0:T(8,128)(2,1)S(1)}, bf16[197,768]{1,0:T(8,128)(2,1)}, u32[]{:S(2)}) copy-start(bf16[197,768]{1,0:T(8,128)(2,1)} %param.12) | copy-start | bytes 907780
  291.8 14.7 %copy-start.27 = (f32[768]{0:T(1024)S(1)}, f32[768]{0:T(1024)}, u32[]{:S(2)}) copy-start(f32[768]{0:T(1024)} %param.13) | copy-start | bytes 9220
  291.8 14.7 %copy-start.30 = (f32[197]{0:T(256)S(1)}, f32[197]{0:T(256)}, u32[]{:S(2)}) copy-start(f32[197]{0:T(256)} %copy-done.29) | copy-start | bytes 2368
  291.8 15.0 %copy-start.38 = (f32[197]{0:T(256)S(1)}, f32[197]{0:T(256)}, u32[]{:S(2)}) copy-start(f32[197]{0:T(256)} %copy-done.37) | copy-start | bytes 2368
  291.8 15.0 %copy-start.33 = (f32[197]{0:T(256)S(1)}, f32[197]{0:T(256)}, u32[]{:S(2)}) copy-start(f32[197]{0:T(256)} %copy-done.32) | copy-start | bytes 2368
  291.8 55.6 %copy-start.8 = (f32[197,768]{1,0:T(8,128)S(1)}, f32[197,768]{1,0:T(8,128)}, u32[]{:S(2)}) copy-start(f32[197,768]{1,0:T(8,128)} %copy-done.7) | copy-start | bytes 1815556
  291.8 12.5 %collective-permute-start.1 = (bf16[3,768]{1,0:T(4,128)(2,1)S(1)}, bf16[3,768]{1,0:T(4,128)(2,1)S(1)}, u32[]{:S(2)}, u32[]{:S(2)}) collective-permute-start(bf16[3,768]{1,0:T(4,128)(2,1)S(1)} %slice.34), channel_id=1, source_target_pairs={{0,1},{2,3},{4,5},{6,7},{8,9},{10,11},{12,13},{14,15},{16,17},{18,... | collective-permute-start | bytes 13832
  582.0 4.1 copy-start.22
  582.0 5.1 copy-start.26
  (11 other events, 11.5 us)
Sparse Core Ops, SparseCore 0:
  87.9 9.0 all-gather.4
  115.8 9.0 all-gather.6
  162.4 8.3 reduce-scatter.6
  192.2 8.5 reduce-scatter.8
  275.0 119.7 all-reduce.9
  401.0 180.9 all-reduce.11
where the time goes:
time: 605 us; the launch traced here: 595 us
  waiting for transfers between devices  292 us (48%)
  matrix products  103 us (17%)
  local copies, waits for them, and re-layouts  68.5 us (11%)
  blocking collectives  53.4 us (9%)
  starting transfers between devices  36.9 us (6%)
  other arithmetic  25.5 us (4%)
  between operations  16.1 us (3%)
    psum x1, waiting for transfers between devices, body(): qkv_grad, out_grad = lax.psum((qkv_grad, out_grad), 'rows')  187 us
    psum x1, waiting for transfers between devices, body(): lax.psum((router_grad, ln1_gain_grad, ln1_shift_grad, ln2_gain_grad, ln2_...  46.3 us
    psum x1, blocking collectives, body(): lax.psum((router_grad, ln1_gain_grad, ln1_shift_grad, ln2_gain_grad, ln2_...  40.2 us
    dot_general x1, matrix products, body(): jnp.dot(both_rows, expert_in, preferred_element_type=jnp.float32) * mask  35.3 us
    unnamed x108, local copies, waits for them, and re-layouts  30.5 us
    dot_general x5, matrix products, dot_rows(): lax.dot_general(first_side, second_side, (((0,), (0,)), ((), ())), prefer...  26.8 us
    dot_general x5, matrix products, dot_last(): lax.dot_general(first_side, second_side, (((1,), (1,)), ((), ())), prefer...  22.5 us
    all_to_all x1, waiting for transfers between devices, body(): lax.all_to_all(grads_send.reshape(row_count, slots, model_width), 'rows',...  18.6 us
  transfers between devices with their start and end apart: 12, of which 7 were waited for; matrix products, arithmetic and copies ran while one was open for 19% of the time, Pallas kernels for 0%

commit v1 on v0

--- a/solution.py
+++ b/solution.py
@@ -247,9 +247,11 @@
     grad_tokens_part, ln1_gain_grad, ln1_shift_grad = norm_one_back(grad_normed)
     tokens_grad = (grad_hidden + grad_tokens_part).astype(jnp.bfloat16)
     qkv_grad, out_grad = lax.psum((qkv_grad, out_grad), "rows")
-    router_grad, ln1_gain_grad, ln1_shift_grad, ln2_gain_grad, ln2_shift_grad = lax.psum(
-        (router_grad, ln1_gain_grad, ln1_shift_grad, ln2_gain_grad, ln2_shift_grad),
-        ("rows", "cols"),
+    cover_tiles_by_axis = lambda field: lax.psum(
+        lax.psum(field, axis_name="cols"), axis_name="rows"
+    )
+    router_grad, ln1_gain_grad, ln1_shift_grad, ln2_gain_grad, ln2_shift_grad = cover_tiles_by_axis(
+        (router_grad, ln1_gain_grad, ln1_shift_grad, ln2_gain_grad, ln2_shift_grad)
     )
     return (
         output,

time: 605 us -> 506 us (0.84)
  waiting for transfers between devices: 292 us -> 152 us
  blocking collectives: 53.4 us -> 94.9 us
    psum x1, waiting for transfers between devices: 187 us -> 77.7 us  [body(): qkv_grad, out_grad = lax.psum((qkv_grad, out_grad), 'rows')]
    psum x1 -> x2, blocking collectives: 40.2 us -> 81.7 us  [the longest x1 78.4 us: body(): lax.psum(lax.psum(field, axis_name='cols'), axis_name='rows')]
    psum x1, waiting for transfers between devices: 46.3 us -> 15.7 us  [body(): lax.psum(field, axis_name='cols')]
  transfers between devices with their start and end apart: 12 -> 12, of which waited for: 7 -> 7; matrix products, arithmetic and copies ran while one was open for 19% -> 23% of each run, Pallas kernels for 0% -> 0%
where the time goes in v1:
time: 506 us; the launch traced here: 497 us
  waiting for transfers between devices  152 us (30%)
  matrix products  103 us (20%)
  blocking collectives  94.9 us (19%)
  local copies, waits for them, and re-layouts  68.5 us (14%)
  starting transfers between devices  36.8 us (7%)
  other arithmetic  25.5 us (5%)
  between operations  16.1 us (3%)
    psum x1, blocking collectives, body(): lax.psum(lax.psum(field, axis_name='cols'), axis_name='rows')  78.4 us
    psum x1, waiting for transfers between devices, body(): qkv_grad, out_grad = lax.psum((qkv_grad, out_grad), 'rows')  77.7 us
    dot_general x1, matrix products, body(): jnp.dot(both_rows, expert_in, preferred_element_type=jnp.float32) * mask  35.3 us
    unnamed x108, local copies, waits for them, and re-layouts  30.6 us
    dot_general x5, matrix products, dot_rows(): lax.dot_general(first_side, second_side, (((0,), (0,)), ((), ())), prefer...  26.8 us
    dot_general x5, matrix products, dot_last(): lax.dot_general(first_side, second_side, (((1,), (1,)), ((), ())), prefer...  22.5 us
    all_to_all x1, waiting for transfers between devices, body(): lax.all_to_all(grads_send.reshape(row_count, slots, model_width), 'rows',...  18.6 us
    psum x1, waiting for transfers between devices, body(): lax.psum(field, axis_name='cols')  15.7 us
  transfers between devices with their start and end apart: 12, of which 7 were waited for; matrix products, arithmetic and copies ran while one was open for 23% of the time, Pallas kernels for 0%

profile of v1, /device:TPU:0, one launch (start us, length us, event | category | flops | bytes accessed | tf_op | source)
XLA Modules:
  0.0 496.6 jit_solution(1925781072087822944)
XLA Ops:
  11.4 2.3 all-gather
  14.9 2.8 reshape.405
  17.7 7.0 %fusion.72 = (bf16[2,197,6,1,64]{4,3,2,1,0:T(2,128)(2,1)S(1)}, bf16[2,197,6,1,64]{4,3,2,1,0:T(2,128)(2,1)}, bf16[2,197,6,1,64]{4,3,2,1,0:T(2,128)(2,1)}) fusion(bf16[2,197,6,3,64]{4,3,2,1,0:T(4,128)(2,1)} %reshape.405), kind=kLoop, calls=%fused_computation.161 | loop fusion | bytes 1815552 | tf_op jit(solution)/shard_map/slice | solution.py:78
  24.7 2.5 copy.120
  27.2 3.7 copy.122
  30.9 2.0 copy.121
  39.8 4.9 fusion
  45.4 2.0 collective-permute-start
  50.8 2.1 concatenate
  56.2 3.9 scatter_custom_fusion
  60.0 8.3 %all-to-all-start = ((bf16[16,32,768]{2,1,0:T(8,128)(2,1)}), bf16[16,32,768]{2,1,0:T(8,128)(2,1)}, u32[]{:S(2)}, u32[]{:S(2)}) async-start(bf16[16,32,768]{2,1,0:T(8,128)(2,1)} %bitcast.8), calls=%async_computation | async-start | bytes 1572864 | tf_op jit(solution)/shard_map/all_to_all | solution.py:129
  69.7 2.1 mul.309
  72.2 15.5 %all-to-all-done = bf16[16,32,768]{2,1,0:T(8,128)(2,1)} async-done(((bf16[16,32,768]{2,1,0:T(8,128)(2,1)}), bf16[16,32,768]{2,1,0:T(8,128)(2,1)}, u32[]{:S(2)}, u32[]{:S(2)}) %all-to-all-start) | async-done | bytes 786464 | tf_op jit(solution)/shard_map/all_to_all | solution.py:129
  88.0 3.2 scatter_custom_fusion.1
  91.2 4.9 all-to-all-start.2
  96.2 18.6 %all-to-all-done.2 = bf16[16,32,768]{2,1,0:T(8,128)(2,1)S(1)} async-done(((bf16[16,32,768]{2,1,0:T(8,128)(2,1)}), bf16[16,32,768]{2,1,0:T(8,128)(2,1)S(1)}, u32[]{:S(2)}, u32[]{:S(2)}) %all-to-all-start.2) | async-done | bytes 786464 | tf_op jit(solution)/shard_map/all_to_all | solution.py:136
  115.8 35.3 %fusion.5 = (bf16[1024,3072]{1,0:T(8,128)(2,1)S(1)}, f32[1024,3072]{1,0:T(8,128)}) fusion(s32[3072]{0:T(1024)S(1)} %add_select_fusion, s32[1024]{0:T(1024)S(1)} %add_select_fusion.1, bf16[1024,768]{1,0:T(8,128)(2,1)} %all-gather.5.cloned.1.call-done, bf16[768,3072]{1,0:T(8,128)(2,1)} %param.20), kind=kOutput, calls=%fused_computation.11 | convolution fusion | flops 5042601984 | bytes 25182208 | tf_op jit(solution)/shard_map/dot_general | solution.py:156
  151.1 2.7 copy-done.44
  153.8 8.5 %convolution_convert_fusion.2 = bf16[1024,768]{1,0:T(8,128)(2,1)} fusion(bf16[1024,3072]{1,0:T(8,128)(2,1)S(1)} %get-tuple-element.42, bf16[3072,768]{1,0:T(8,128)(2,1)} %param.21), kind=kOutput, calls=%fused_computation.39 | convolution fusion | flops 4832624640 | bytes 12582912 | tf_op jit(solution)/shard_map/dot_general | solution.py:159
  162.3 8.7 %reduce-scatter.9.cloned.1.call-start = ((), (), s32[]{:S(2)}) async-start(), calls=%async_computation.9 | async-start | bytes 2359296 | tf_op jit(solution)/shard_map/reduce_scatter | solution.py:168
  171.1 12.0 %fusion.2 = bf16[1024,3072]{1,0:T(8,128)(2,1)S(1)} fusion(f32[1024,3072]{1,0:T(8,128)} %get-tuple-element.43, bf16[1024,768]{1,0:T(8,128)(2,1)} %all-gather.7.cloned.1.call-done, bf16[3072,768]{1,0:T(8,128)(2,1)} %param.21, s32[3072]{0:T(1024)S(1)} %add_select_fusion, s32[1024]{0:T(1024)S(1)} %add_select_fusion.1), kind=kOutput, calls=%fused_computation.8 | convolution fusion | flops 4872732672 | bytes 25182208 | tf_op jit(solution)/shard_map/dot_general | solution.py:32
  183.1 2.7 copy-done.43
  185.8 6.3 %convolution_convert_fusion.1 = bf16[1024,768]{1,0:T(8,128)(2,1)} fusion(bf16[1024,3072]{1,0:T(8,128)(2,1)S(1)} %fusion.2, bf16[768,3072]{1,0:T(8,128)(2,1)S(1)} %bitcast.115), kind=kOutput, calls=%fused_computation.38 | convolution fusion | flops 4832624640 | bytes 12582912 | tf_op jit(solution)/shard_map/dot_general | solution.py:32
  192.1 5.2 %all-to-all-start.1 = ((bf16[16,32,768]{2,1,0:T(8,128)(2,1)}), bf16[16,32,768]{2,1,0:T(8,128)(2,1)S(1)}, u32[]{:S(2)}, u32[]{:S(2)}) async-start(bf16[16,32,768]{2,1,0:T(8,128)(2,1)} %bitcast.109), calls=%async_computation.2 | async-start | bytes 1572864 | tf_op jit(solution)/shard_map/all_to_all | solution.py:174
  197.2 3.5 reduce-scatter.9.cloned.1.call-done
  200.8 15.2 %all-to-all-done.1 = bf16[16,32,768]{2,1,0:T(8,128)(2,1)S(1)} async-done(((bf16[16,32,768]{2,1,0:T(8,128)(2,1)}), bf16[16,32,768]{2,1,0:T(8,128)(2,1)S(1)}, u32[]{:S(2)}, u32[]{:S(2)}) %all-to-all-start.1) | async-done | bytes 786464 | tf_op jit(solution)/shard_map/all_to_all | solution.py:174
  216.0 4.9 all-to-all-start.3
  222.8 2.6 gather_fusion
  225.4 2.8 reshape.365
  228.2 4.7 multiply_reduce_fusion.2
  234.1 5.3 %all-to-all-done.3 = bf16[16,32,768]{2,1,0:T(8,128)(2,1)S(1)} async-done(((bf16[16,32,768]{2,1,0:T(8,128)(2,1)}), bf16[16,32,768]{2,1,0:T(8,128)(2,1)S(1)}, u32[]{:S(2)}, u32[]{:S(2)}) %all-to-all-start.3) | async-done | bytes 786464 | tf_op jit(solution)/shard_map/all_to_all | solution.py:187
  239.5 2.6 gather_fusion.1
  242.1 2.8 reshape.366
  245.0 2.7 reduce_sum.212
  249.8 2.0 fusion.70
  252.8 2.6 all-gather.1
  260.9 3.2 fusion.22
  270.2 4.6 fusion.75
  276.4 15.7 %all-reduce.11.cloned.1.call-done = f32[768,32]{0,1:T(8,128)} async-done(((f32[768,32]{0,1:T(8,128)}), f32[768,32]{0,1:T(8,128)}) %all-reduce.11.cloned.1.call-update) | async-done | bytes 98320 | tf_op jit(solution)/shard_map/psum | solution.py:251
  292.1 10.0 %fusion.79 = f32[3072,768]{1,0:T(8,128)} fusion(bf16[1024,3072]{1,0:T(8,128)(2,1)} %copy-done.44, bf16[1024,768]{1,0:T(8,128)(2,1)} %all-gather.7.cloned.1.call-done), kind=kOutput, calls=%fused_computation.168 | convolution fusion | flops 4831838208 | bytes 17301504 | tf_op jit(solution)/shard_map/dot_general | solution.py:26
  303.4 3.4 fusion.1
  307.6 2.6 collective-permute-start.1
  310.2 9.9 %fusion.78 = f32[768,3072]{1,0:T(8,128)} fusion(bf16[1024,768]{1,0:T(8,128)(2,1)} %all-gather.5.cloned.1.call-done, bf16[1024,3072]{1,0:T(8,128)(2,1)} %copy-done.43), kind=kOutput, calls=%fused_computation.167 | convolution fusion | flops 4831838208 | bytes 17301504 | tf_op jit(solution)/shard_map/dot_general | solution.py:26
  320.1 2.0 concatenate.1
  323.0 3.3 all-reduce.7
  326.3 78.4 %all-reduce.5 = (f32[768]{0:T(1024)}, f32[768]{0:T(1024)}, f32[768]{0:T(1024)}, f32[768]{0:T(1024)}) all-reduce(f32[768]{0:T(1024)S(1)} %get-tuple-element.26, f32[768]{0:T(1024)S(1)} %get-tuple-element.27, f32[768]{0:T(1024)S(1)} %get-tuple-element.28, f32[768]{0:T(1024)S(1)} %get-tuple-element.29), channel_id=1, replica_groups=mesh['rows'=16,'cols'=2] {'rows'}, use_global_device_ids=true, to_apply=%region_30.31 | all-reduce | flops 3072 | bytes 24576 | tf_op jit(solution)/shard_map/psum | solution.py:250
  405.7 77.7 %all-reduce.13.cloned.1.call-done = (f32[768,1152]{1,0:T(8,128)}, f32[384,768]{1,0:T(8,128)}, f32[768,32]{0,1:T(8,128)}) async-done(((f32[768,1152]{1,0:T(8,128)}, f32[384,768]{1,0:T(8,128)}, f32[768,32]{0,1:T(8,128)}), (f32[768,1152]{1,0:T(8,128)}, f32[384,768]{1,0:T(8,128)}, f32[768,32]{0,1:T(8,128)})) %all-reduce.13.cloned.1.call-update) | async-done | bytes 4816912 | tf_op jit(solution)/shard_map/psum | solution.py:249
  483.5 4.1 copy.131
  (186 shorter events, 46.5 us)
Async XLA Ops:
  7.2 6.7 %copy-start = (bf16[768,1152]{1,0:T(8,128)(2,1)S(1)}, bf16[768,1152]{1,0:T(8,128)(2,1)}, u32[]{:S(2)}) copy-start(bf16[768,1152]{1,0:T(8,128)(2,1)} %param.15) | copy-start | bytes 5308420
  8.4 3.0 copy-start.29
  27.2 9.4 %copy-start.13 = (bf16[2,197,6,1,64]{1,4,2,0,3:T(8,128)(2,1)}, bf16[2,197,6,1,64]{1,4,2,0,3:T(8,128)(2,1)S(1)}, u32[]{:S(2)}) copy-start(bf16[2,197,6,1,64]{1,4,2,0,3:T(8,128)(2,1)S(1)} %copy.120) | copy-start | bytes 907780
  35.1 12.4 %copy-start.31 = (s32[197,2]{0,1:T(2,128)S(1)}, s32[197,2]{0,1:T(2,128)}, u32[]{:S(2)}) copy-start(s32[197,2]{0,1:T(2,128)} %param.22) | copy-start | bytes 4732
  36.0 13.5 %copy-start.42 = (u32[32]{0:T(128)S(1)}, u32[32]{0:T(128)}, u32[]{:S(2)}) copy-start(u32[32]{0:T(128)} %constant.193) | copy-start | bytes 388
  36.0 16.9 %copy-start.5 = (bf16[197,768]{1,0:T(8,128)(2,1)S(1)}, bf16[197,768]{1,0:T(8,128)(2,1)}, u32[]{:S(2)}) copy-start(bf16[197,768]{1,0:T(8,128)(2,1)} %param.12) | copy-start | bytes 907780
  37.1 16.9 %copy-start.28 = (f32[768]{0:T(1024)S(1)}, f32[768]{0:T(1024)}, u32[]{:S(2)}) copy-start(f32[768]{0:T(1024)} %param.17) | copy-start | bytes 9220
  37.1 16.9 %copy-start.41 = (f32[768]{0:T(1024)S(1)}, f32[768]{0:T(1024)}, u32[]{:S(2)}) copy-start(f32[768]{0:T(1024)} %param.18) | copy-start | bytes 9220
  45.4 5.4 %collective-permute-start = (f32[3,768]{1,0:T(4,128)S(1)}, f32[3,768]{1,0:T(4,128)S(1)}, u32[]{:S(2)}, u32[]{:S(2)}) collective-permute-start(f32[3,768]{1,0:T(4,128)S(1)} %slice.33), channel_id=1, source_target_pairs={{0,1},{2,3},{4,5},{6,7},{8,9},{10,11},{12,13},{14,15},{16,17},{18,... | collective-permute-start | bytes 27656
  47.9 20.5 %copy-start.9 = (bf16[197,768]{1,0:T(8,128)(2,1)S(1)}, bf16[197,768]{1,0:T(8,128)(2,1)}, u32[]{:S(2)}) copy-start(bf16[197,768]{1,0:T(8,128)(2,1)} %param.23) | copy-start | bytes 907780
  53.4 18.8 %copy-start.39 = (f32[197]{0:T(256)}, f32[197]{0:T(256)S(1)}, u32[]{:S(2)}) copy-start(f32[197]{0:T(256)S(1)} %multiply_reduce_fusion.6) | copy-start | bytes 2368
  53.4 18.5 %copy-start.25 = (bf16[768,32]{0,1:T(8,128)(2,1)S(1)}, bf16[768,32]{0,1:T(8,128)(2,1)}, u32[]{:S(2)}) copy-start(bf16[768,32]{0,1:T(8,128)(2,1)} %param.19) | copy-start | bytes 147460
  53.9 18.2 %copy-start.34 = (f32[197]{0:T(256)}, f32[197]{0:T(256)S(1)}, u32[]{:S(2)}) copy-start(f32[197]{0:T(256)S(1)} %fusion.67) | copy-start | bytes 2368
  54.1 33.6 %copy-start.11 = (bf16[197,768]{1,0:T(8,128)(2,1)}, bf16[197,768]{1,0:T(8,128)(2,1)S(1)}, u32[]{:S(2)}) copy-start(bf16[197,768]{1,0:T(8,128)(2,1)S(1)} %add_convert_fusion.2) | copy-start | bytes 907780
  60.0 27.7 %all-to-all-start = ((bf16[16,32,768]{2,1,0:T(8,128)(2,1)}), bf16[16,32,768]{2,1,0:T(8,128)(2,1)}, u32[]{:S(2)}, u32[]{:S(2)}) async-start(bf16[16,32,768]{2,1,0:T(8,128)(2,1)} %bitcast.8), calls=%async_computation | async-start | bytes 1572864 | tf_op jit(solution)/shard_map/all_to_all | solution.py:129
  68.3 47.4 %all-gather.5.cloned.1.call-start = ((), (), s32[]{:S(2)}) async-start(), calls=%async_computation.6 | async-start | bytes 2359296 | tf_op jit(solution)/shard_map/all_gather | solution.py:148
  72.2 15.5 %copy-start.36 = (f32[197]{0:T(256)}, f32[197]{0:T(256)S(1)}, u32[]{:S(2)}) copy-start(f32[197]{0:T(256)S(1)} %fusion.55) | copy-start | bytes 2368
  91.2 23.5 %all-to-all-start.2 = ((bf16[16,32,768]{2,1,0:T(8,128)(2,1)}), bf16[16,32,768]{2,1,0:T(8,128)(2,1)S(1)}, u32[]{:S(2)}, u32[]{:S(2)}) async-start(bf16[16,32,768]{2,1,0:T(8,128)(2,1)} %bitcast.107), calls=%async_computation.3 | async-start | bytes 1572864 | tf_op jit(solution)/shard_map/all_to_all | solution.py:136
  96.1 74.9 %all-gather.7.cloned.1.call-start = ((), (), s32[]{:S(2)}) async-start(), calls=%async_computation.8 | async-start | bytes 2359296 | tf_op jit(solution)/shard_map/all_gather | solution.py:149
  115.7 76.4 %reduce-scatter.7.cloned.1.call-start = ((), (), s32[]{:S(2)}) async-start(), calls=%async_computation.7 | async-start | bytes 2359296 | tf_op jit(solution)/shard_map/reduce_scatter | solution.py:158
  151.0 2.7 copy-start.44
  153.8 32.0 %slice-start = ((s8[4718592]{0:T(1024)(128)(4,1)}), s8[524288]{0:T(1024)(128)(4,1)S(1)}, s32[]{:S(2)}) async-start(s8[4718592]{0:T(1024)(128)(4,1)} %bitcast.114), calls=%async_computation.12 | async-start | bytes 1048576
  162.3 38.5 %reduce-scatter.9.cloned.1.call-start = ((), (), s32[]{:S(2)}) async-start(), calls=%async_computation.9 | async-start | bytes 2359296 | tf_op jit(solution)/shard_map/reduce_scatter | solution.py:168
  171.1 14.7 %slice-start.1 = ((s8[4718592]{0:T(1024)(128)(4,1)}), s8[4194304]{0:T(1024)(128)(4,1)S(1)}, s32[]{:S(2)}) async-start(s8[4718592]{0:T(1024)(128)(4,1)} %bitcast.114), calls=%async_computation.13 | async-start | bytes 8388608
  183.1 2.7 copy-start.43
  192.1 23.9 %all-to-all-start.1 = ((bf16[16,32,768]{2,1,0:T(8,128)(2,1)}), bf16[16,32,768]{2,1,0:T(8,128)(2,1)S(1)}, u32[]{:S(2)}, u32[]{:S(2)}) async-start(bf16[16,32,768]{2,1,0:T(8,128)(2,1)} %bitcast.109), calls=%async_computation.2 | async-start | bytes 1572864 | tf_op jit(solution)/shard_map/all_to_all | solution.py:174
  216.0 23.5 %all-to-all-start.3 = ((bf16[16,32,768]{2,1,0:T(8,128)(2,1)}), bf16[16,32,768]{2,1,0:T(8,128)(2,1)S(1)}, u32[]{:S(2)}, u32[]{:S(2)}) async-start(bf16[16,32,768]{2,1,0:T(8,128)(2,1)} %bitcast.108), calls=%async_computation.5 | async-start | bytes 1572864 | tf_op jit(solution)/shard_map/all_to_all | solution.py:187
  220.9 71.3 %all-reduce.11.cloned.1.call-start = ((), (), s32[]{:S(2)}) async-start(), calls=%async_computation.10 | async-start | bytes 196608 | tf_op jit(solution)/shard_map/psum | solution.py:251
  232.8 15.6 %copy-start.4 = (f32[197,768]{1,0:T(8,128)S(1)}, f32[197,768]{1,0:T(8,128)}, u32[]{:S(2)}) copy-start(f32[197,768]{1,0:T(8,128)} %copy-done.3) | copy-start | bytes 1815556
  242.1 7.6 %copy-start.40 = (f32[197]{0:T(256)S(1)}, f32[197]{0:T(256)}, u32[]{:S(2)}) copy-start(f32[197]{0:T(256)} %copy-done.39) | copy-start | bytes 2368
  242.1 7.7 %copy-start.35 = (f32[197]{0:T(256)S(1)}, f32[197]{0:T(256)}, u32[]{:S(2)}) copy-start(f32[197]{0:T(256)} %copy-done.34) | copy-start | bytes 2368
  242.1 10.5 %copy-start.10 = (bf16[197,768]{1,0:T(8,128)(2,1)S(1)}, bf16[197,768]{1,0:T(8,128)(2,1)}, u32[]{:S(2)}) copy-start(bf16[197,768]{1,0:T(8,128)(2,1)} %param.23) | copy-start | bytes 907780
  252.8 11.3 %copy-start.14 = (bf16[2,197,6,1,64]{1,4,2,0,3:T(8,128)(2,1)S(1)}, bf16[2,197,6,1,64]{1,4,2,0,3:T(8,128)(2,1)}, u32[]{:S(2)}) copy-start(bf16[2,197,6,1,64]{1,4,2,0,3:T(8,128)(2,1)} %copy-done.13) | copy-start | bytes 907780
  260.9 3.2 copy-start.2
  264.9 2.3 copy-start.20
  270.2 4.7 copy-start.17
  270.2 4.7 copy-start.19
  274.9 208.6 %all-reduce.13.cloned.1.call-start = ((), (), s32[]{:S(2)}) async-start(), calls=%async_computation.11 | async-start | bytes 9633792 | tf_op jit(solution)/shard_map/psum | solution.py:249
  292.1 10.0 %copy-start.23 = (bf16[394,1152]{0,1:T(8,128)(2,1)S(1)}, bf16[394,1152]{0,1:T(8,128)(2,1)}, u32[]{:S(2)}) copy-start(bf16[394,1152]{0,1:T(8,128)(2,1)} %convert_element_type.115) | copy-start | bytes 2723332
  307.5 14.6 %copy-start.6 = (bf16[197,768]{1,0:T(8,128)(2,1)S(1)}, bf16[197,768]{1,0:T(8,128)(2,1)}, u32[]{:S(2)}) copy-start(bf16[197,768]{1,0:T(8,128)(2,1)} %param.12) | copy-start | bytes 907780
  307.5 14.6 %copy-start.27 = (f32[768]{0:T(1024)S(1)}, f32[768]{0:T(1024)}, u32[]{:S(2)}) copy-start(f32[768]{0:T(1024)} %param.13) | copy-start | bytes 9220
  307.6 14.6 %copy-start.30 = (f32[197]{0:T(256)S(1)}, f32[197]{0:T(256)}, u32[]{:S(2)}) copy-start(f32[197]{0:T(256)} %copy-done.29) | copy-start | bytes 2368
  307.6 14.9 %copy-start.38 = (f32[197]{0:T(256)S(1)}, f32[197]{0:T(256)}, u32[]{:S(2)}) copy-start(f32[197]{0:T(256)} %copy-done.37) | copy-start | bytes 2368
  307.6 14.9 %copy-start.33 = (f32[197]{0:T(256)S(1)}, f32[197]{0:T(256)}, u32[]{:S(2)}) copy-start(f32[197]{0:T(256)} %copy-done.32) | copy-start | bytes 2368
  307.6 97.1 %copy-start.8 = (f32[197,768]{1,0:T(8,128)S(1)}, f32[197,768]{1,0:T(8,128)}, u32[]{:S(2)}) copy-start(f32[197,768]{1,0:T(8,128)} %copy-done.7) | copy-start | bytes 1815556
  307.6 12.5 %collective-permute-start.1 = (bf16[3,768]{1,0:T(4,128)(2,1)S(1)}, bf16[3,768]{1,0:T(4,128)(2,1)S(1)}, u32[]{:S(2)}, u32[]{:S(2)}) collective-permute-start(bf16[3,768]{1,0:T(4,128)(2,1)S(1)} %slice.34), channel_id=1, source_target_pairs={{0,1},{2,3},{4,5},{6,7},{8,9},{10,11},{12,13},{14,15},{16,17},{18,... | collective-permute-start | bytes 13832
  483.5 4.1 copy-start.22
  483.5 5.1 %copy-start.26 = (f32[768,32]{0,1:T(8,128)S(1)}, f32[768,32]{0,1:T(8,128)}, u32[]{:S(2)}) copy-start(f32[768,32]{0,1:T(8,128)} %get-tuple-element.55) | copy-start | bytes 294916
  (11 other events, 11.5 us)
Sparse Core Ops, SparseCore 0:
  87.9 9.0 all-gather.4
  115.8 9.0 all-gather.6
  162.4 8.3 reduce-scatter.6
  192.2 8.5 reduce-scatter.8
  275.0 17.0 all-reduce.10
  298.7 184.7 all-reduce.12
